TPU v7x, 128 devices: a whole 4x4x4 slice. The times are simulated.
128 devices in a mesh: seq: 16 (over z, y), head: 8 (over x, core).
Axes of the slice: x: 4, y: 4, z: 4, core: 2. Of those that a mesh axis runs over, the one named last changes fastest.
Arguments:
- normed: bfloat16 [32, 8192], P(None, 'seq'), may hold values from -6 to 6
- qkv_weight: bfloat16 [8192, 10240], P('seq', 'head'), may hold values from -0.0625 to 0.0625
- out_weight: bfloat16 [8192, 8192], P('head', 'seq'), may hold values from -0.0625 to 0.0625
- kv_cache: bfloat16 [1024, 2, 128, 1024], P('seq', None, None, 'head'), may hold values from -160 to 160
- lengths: int32 [8], replicated, may hold values from 1 to 9344, as said below
- slot_request: int32 [1024], P('seq'), may hold values from 0 to 8, as said below
- slot_block: int32 [1024], P('seq'), may hold values from 0 to 72, as said below
- send_list: int32 [16, 16, 4], P('seq'), may hold values from 0 to 64, as said below
- recv_list: int32 [16, 16, 4], P('seq'), may hold values from 0 to 64, as said below
Outputs:
- projected: bfloat16 [32, 8192], P('head', 'seq')
- moved_cache: bfloat16 [1024, 2, 128, 1024], P('seq', None, None, 'head')
Inputs may be any that keep to these rules, and one draw needn't show every extreme that they name: `lengths`: every request has at least one block; a request with n blocks has each of the block numbers 0 to n - 1 in exactly one slot, and its length lies in ((n - 1) * 128, n * 128]. `slot_request`: 8 marks an empty slot. `slot_block`: 0 in empty slots. 64 marks an unused entry, and send_list[s, e, c] is unused exactly where recv_list[e, s, c] is; every owned slot is sent exactly once and no empty slot is sent; at most 4 blocks go from one device to another, and some device receives exactly 4 from every device; after the scale-in only half of the seq devices hold blocks. `recv_list`: 64 marks an unused entry; each slot of a device is filled at most once.
All inputs are finite; a program needn't handle non-finite values.
Results may differ from a plain program's by a relative error of at most 0.025.
Values may be sent and summed in bfloat16 or wider, within the bound.
A program may use at most 128 MiB of HBM per device.

v0:
```python
import jax
import jax.numpy as jnp
from jax import lax
from jax.sharding import PartitionSpec as P

HEADS = 64
KV_HEADS = 8
HEAD = 128
POS = 4
BLOCK = 128


rope_base = 500000.0
neg_large = -1e30


def rotate(values, positions):
    half_width = values.shape[-1] // 2
    frequencies = rope_base ** (
        -(jnp.arange(half_width, dtype=jnp.float32) * 2.0 / values.shape[-1])
    )
    angles = positions[..., None] * frequencies
    cosine_table = jnp.cos(angles)
    sine_table = jnp.sin(angles)
    lower_half = values[..., :half_width]
    upper_half = values[..., half_width:]
    return jnp.concatenate(
        [
            lower_half * cosine_table - upper_half * sine_table,
            upper_half * cosine_table + lower_half * sine_table,
        ],
        axis=-1,
    )


def body(
    normed,
    qkv_weight,
    out_weight,
    kv_cache,
    lengths,
    slot_request,
    slot_block,
    send_list,
    recv_list,
):
    group_size = HEADS // KV_HEADS
    scale_factor = HEAD ** (-0.5)
    requests = lengths.shape[0]
    slot_count = kv_cache.shape[0]
    full_rows = lax.all_gather(normed, "seq", axis=1, tiled=True)
    projected_qkv = jnp.dot(
        full_rows,
        lax.all_gather(qkv_weight, "seq", axis=0, tiled=True),
        preferred_element_type=jnp.float32,
    )
    projected_qkv = projected_qkv.reshape(requests, POS, -1, group_size + 2, HEAD)
    local_kv = projected_qkv.shape[2]
    positions = (lengths[:, None] + jnp.arange(POS, dtype=jnp.int32)[None, :]).astype(jnp.float32)
    queries = rotate(projected_qkv[:, :, :, :group_size], positions[:, :, None, None]).astype(
        jnp.bfloat16
    )
    keys_new = rotate(projected_qkv[:, :, :, group_size], positions[:, :, None]).astype(
        jnp.bfloat16
    )
    values_new = projected_qkv[:, :, :, group_size + 1].astype(jnp.bfloat16)
    flat_send = send_list.reshape(-1)
    outgoing = kv_cache[jnp.minimum(flat_send, slot_count - 1)]
    outgoing = outgoing.reshape((lax.axis_size("seq"), -1) + kv_cache.shape[1:])
    incoming = lax.all_to_all(outgoing, "seq", split_axis=0, concat_axis=0, tiled=True)
    incoming = incoming.reshape((-1,) + kv_cache.shape[1:])
    moved_cache = jnp.zeros_like(kv_cache).at[recv_list.reshape(-1)].set(incoming, mode="drop")
    slot_clip = jnp.minimum(slot_request, requests - 1)
    live_slot = slot_request < requests
    token_pos = slot_block[:, None] * BLOCK + jnp.arange(BLOCK, dtype=jnp.int32)[None, :]
    token_valid = (token_pos < lengths[slot_clip][:, None]) & live_slot[:, None]
    cache_view = kv_cache.reshape(slot_count, 2, BLOCK, local_kv, HEAD)
    gathered = queries[slot_clip]
    scores = (
        jnp.einsum(
            "sptgd,sbtd->stgpb", gathered, cache_view[:, 0], preferred_element_type=jnp.float32
        )
        * scale_factor
    )
    scores = jnp.where(token_valid[:, None, None, None, :], scores, neg_large)
    slot_max = jnp.max(scores, axis=-1)
    weights = jnp.where(
        token_valid[:, None, None, None, :], jnp.exp(scores - slot_max[..., None]), 0.0
    )
    slot_sum = jnp.sum(weights, axis=-1)
    slot_acc = jnp.einsum(
        "stgpb,sbtd->stgpd",
        weights.astype(jnp.bfloat16),
        cache_view[:, 1],
        preferred_element_type=jnp.float32,
    )
    flat_width = local_kv * group_size * POS
    slot_max_flat = slot_max.reshape(slot_count, flat_width)
    member = slot_request[:, None] == jnp.arange(requests, dtype=jnp.int32)[None, :]
    request_max = jnp.max(
        jnp.where(member[:, None, :], slot_max_flat[:, :, None], neg_large), axis=0
    ).T
    rescale = jnp.exp(slot_max_flat - request_max[slot_clip])
    member_float = member.astype(jnp.float32).T
    request_sum = jnp.dot(
        member_float,
        slot_sum.reshape(slot_count, flat_width) * rescale,
        precision=lax.Precision.HIGHEST,
    )
    scaled_acc = (slot_acc.reshape(slot_count, flat_width, HEAD) * rescale[:, :, None]).reshape(
        slot_count, flat_width * HEAD
    )
    request_acc = jnp.dot(member_float, scaled_acc, precision=lax.Precision.HIGHEST).reshape(
        requests, flat_width, HEAD
    )
    total_max = lax.pmax(request_max, "seq")
    adjust = jnp.exp(request_max - total_max)
    total_sum, total_acc = (
        lax.psum((request_sum * adjust).astype(jnp.bfloat16), "seq").astype(jnp.float32),
        lax.psum((request_acc * adjust[:, :, None]).astype(jnp.bfloat16), "seq").astype(
            jnp.float32
        ),
    )
    new_scores = (
        jnp.einsum("rptgd,rqtd->rtgpq", queries, keys_new, preferred_element_type=jnp.float32)
        * scale_factor
    )
    causal = jnp.arange(POS)[:, None] >= jnp.arange(POS)[None, :]
    new_scores = jnp.where(causal, new_scores, neg_large)
    cache_max = total_max.reshape(requests, local_kv, group_size, POS)
    top_max = jnp.maximum(cache_max, jnp.max(new_scores, axis=-1))
    carry_scale = jnp.exp(cache_max - top_max)
    new_weights = jnp.where(causal, jnp.exp(new_scores - top_max[..., None]), 0.0)
    denominator = total_sum.reshape(requests, local_kv, group_size, POS) * carry_scale + jnp.sum(
        new_weights, axis=-1
    )
    numerator = (
        total_acc.reshape(requests, local_kv, group_size, POS, HEAD) * carry_scale[..., None]
    )
    numerator = numerator + jnp.einsum(
        "rtgpq,rqtd->rtgpd",
        new_weights.astype(jnp.bfloat16),
        values_new,
        preferred_element_type=jnp.float32,
    )
    attended = (
        (numerator / denominator[..., None])
        .transpose(0, 3, 1, 2, 4)
        .reshape(requests * POS, -1)
        .astype(jnp.bfloat16)
    )
    projected = lax.psum_scatter(
        jnp.dot(attended, out_weight, preferred_element_type=jnp.float32).astype(jnp.bfloat16),
        "head",
        scatter_dimension=0,
        tiled=True,
    )
    return (projected, moved_cache)


def solution(mesh):
    placed = (
        P(None, "seq"),
        P("seq", "head"),
        P("head", "seq"),
        P("seq", None, None, "head"),
        P(),
        P("seq"),
        P("seq"),
        P("seq", None, None),
        P("seq", None, None),
    )
    return jax.shard_map(
        body,
        mesh=mesh,
        in_specs=placed,
        out_specs=(P("head", "seq"), P("seq", None, None, "head")),
        check_vma=False,
    )
```

profile of v0, /device:TPU:1, one launch (start us, length us, event | category | flops | bytes accessed | tf_op | source)
XLA Modules:
  0.0 361.5 jit_solution(1940336600849006869)
XLA Ops:
  7.2 0.7 all-gather.2.cloned.1.call-update
  7.9 0.7 broadcast_minimum_fusion
  8.7 0.1 min.26
  8.8 5.3 %gather_fusion.2 = bf16[64,2,128,128]{3,2,1,0:T(8,128)(2,1)} fusion(bf16[64,2,128,128]{3,2,1,0:T(8,128)(2,1)} %param.12, s32[1024]{0:T(1024)S(1)} %pad_clamp_fusion), kind=kCustom, calls=%fused_computation.2 | custom fusion | bytes 8388864 | tf_op jit(solution)/shard_map/gather | solution.py:68
  14.1 8.6 %all-to-all-start = ((bf16[16,4,2,128,128]{4,3,2,1,0:T(8,128)(2,1)}), bf16[16,4,2,128,128]{4,3,2,1,0:T(8,128)(2,1)}, u32[]{:S(2)}, u32[]{:S(2)}) async-start(bf16[16,4,2,128,128]{4,3,2,1,0:T(8,128)(2,1)} %bitcast.134), calls=%async_computation | async-start | bytes 8388608 | tf_op jit(solution)/shard_map/all_to_all | solution.py:70
  22.9 5.3 %copy.111 = bf16[64,2,128,128]{3,2,0,1:T(8,128)(2,1)} copy(bf16[64,2,128,128]{3,2,1,0:T(8,128)(2,1)} %param.12) | data formatting | bytes 8388608 | tf_op args[3]
  28.3 0.1 reshape.425
  28.4 0.6 dynamic-slice
  29.6 0.6 iota_compare_fusion.3
  30.2 0.7 fusion.53
  30.9 4.8 %compare_select_fusion.3 = (s32[64]{0:T(128)S(1)}, s32[64]{0:T(128)S(1)}, s32[64]{0:T(128)S(1)}) fusion(s32[]{:T(128)} %bitcast.1, s32[]{:T(128)} %bitcast.2, s32[]{:T(128)} %bitcast.3, s32[]{:T(128)} %bitcast.4, s32[]{:T(128)} %bitcast.5, s32[]{:T(128)} %bitcast.6, s32[]{:T(128)} %bitcast.7, s32[]{:T(128)} %bitcast.8, s32[64]{0:T(128)S(1)} %copy-done.7, ...), kind=kLoop, calls=%fused_computation.87 | loop fusion | flops 1216 | bytes 1312 | tf_op jit(solution)/shard_map/gather | solution.py:76
  35.7 76.0 %all_gather.6 = bf16[32,8192]{1,0:T(8,128)(2,1)S(1)} all-gather(bf16[32,512]{1,0:T(8,128)(2,1)S(1)} %copy-done.6), channel_id=1, replica_groups=mesh['seq'=16,'head'=8] {'seq'}, dimensions={1}, use_global_device_ids=true | all-gather | bytes 557056 | tf_op jit(solution)/shard_map/all_gather | solution.py:51
  111.8 0.1 fusion.31
  111.9 0.2 multiply_cosine_fusion.1
  112.1 3.1 broadcast_in_dim.96
  115.2 11.8 %scatter_fusion = bf16[64,2,128,128]{3,2,1,0:T(8,128)(2,1)} fusion(bf16[64,2,128,128]{3,2,1,0:T(8,128)(2,1)} %broadcast_in_dim.96, s32[64]{0:T(128)S(1)} %fusion.49, bf16[64,2,128,128]{3,2,1,0:T(8,128)(2,1)} %bitcast.45), kind=kCustom, calls=%fused_computation.3 | custom fusion | bytes 12583168 | tf_op jit(solution)/shard_map/scatter | solution.py:72
  127.0 65.8 %all-gather.2.cloned.1.call-done = bf16[8192,1280]{1,0:T(8,128)(2,1)} async-done(((bf16[512,1280]{1,0:T(8,128)(2,1)}), bf16[8192,1280]{1,0:T(8,128)(2,1)}) %all-gather.2.cloned.1.call-update) | async-done | bytes 20971536 | tf_op jit(solution)/shard_map/all_gather | solution.py:54
  192.8 8.8 %fusion.56 = f32[32,1280]{1,0:T(8,128)S(1)} fusion(bf16[32,8192]{1,0:T(8,128)(2,1)S(1)} %all_gather.6, bf16[8192,1280]{1,0:T(8,128)(2,1)} %all-gather.2.cloned.1.call-done), kind=kOutput, calls=%fused_computation.106 | convolution fusion | flops 671088640 | bytes 21659648 | tf_op jit(solution)/shard_map/dot_general | solution.py:52
  201.7 0.1 subtract_convert_fusion
  201.8 0.1 maximum_bitcast_fusion
  201.9 0.7 gather_fusion
  202.6 2.9 fusion.54
  205.6 0.7 copy.66
  206.3 0.1 select_reduce_fusion
  206.5 30.9 %pmax.7 = f32[8,32]{1,0:T(8,128)S(1)} all-reduce(f32[8,32]{1,0:T(8,128)S(1)} %bitcast.130), channel_id=1, replica_groups=mesh['seq'=16,'head'=8] {'seq'}, use_global_device_ids=true, to_apply=%region_2.3 | all-reduce | flops 256 | bytes 2048 | tf_op jit(solution)/shard_map/pmax | solution.py:116
  237.4 1.2 gather_fusion.1
  238.6 0.7 copy.70
  239.3 0.7 copy.68
  240.0 0.7 fusion.15
  240.7 2.3 fusion
  243.0 0.4 reshape.416
  243.4 0.8 subtract_exponential_fusion
  244.2 0.3 mul.180
  244.6 1.8 fusion.7
  246.4 0.7 copy.69
  247.0 0.9 fusion.45
  247.9 0.8 copy.73
  248.9 0.8 fusion.11
  249.7 0.1 copy.78
  249.8 0.1 copy.79
  249.9 29.0 %psum.15 = bf16[8,8,4]{1,2,0:T(4,128)(2,1)S(1)} all-reduce(bf16[8,8,4]{1,2,0:T(4,128)(2,1)S(1)} %copy.79), channel_id=1, replica_groups=mesh['seq'=16,'head'=8] {'seq'}, use_global_device_ids=true, to_apply=%region_6.7 | all-reduce | flops 256 | bytes 1024 | tf_op jit(solution)/shard_map/psum | solution.py:119
  279.0 1.4 fusion.55
  280.4 0.1 fusion.24
  280.6 49.3 %all-reduce.3.cloned.1.call-done = bf16[8,8,4,128]{3,1,2,0:T(8,128)(2,1)} async-done(((bf16[8,8,4,128]{3,1,2,0:T(8,128)(2,1)}), bf16[8,8,4,128]{3,1,2,0:T(8,128)(2,1)}) %all-reduce.3.cloned.1.call-update) | async-done | bytes 65552 | tf_op jit(solution)/shard_map/psum | solution.py:120
  329.9 1.1 fusion.8
  331.0 0.3 convolution_convert_fusion
  331.3 22.7 %all-reduce = bf16[32,512]{1,0:T(8,128)(2,1)S(1)} all-reduce(bf16[32,512]{1,0:T(8,128)(2,1)S(1)} %convolution_convert_fusion), channel_id=2, replica_groups=mesh['seq'=16,'head'=8] {'head'}, use_global_device_ids=true, to_apply=%region_8.9.clone | all-reduce | flops 16384 | bytes 65536
  354.0 0.6 constant_dynamic-slice_fusion
  (51 shorter events, 0.9 us)
Async XLA Ops:
  7.2 323.9 %copy-start = (bf16[1024,512]{1,0:T(8,128)(2,1)S(1)}, bf16[1024,512]{1,0:T(8,128)(2,1)}, u32[]{:S(2)}) copy-start(bf16[1024,512]{1,0:T(8,128)(2,1)} %param.11) | copy-start | bytes 3145732
  7.2 185.7 %all-gather.2.cloned.1.call-start = ((), (), s32[]{:S(2)}) async-start(), calls=%async_computation.1 | async-start | bytes 22282240 | tf_op jit(solution)/shard_map/all_gather | solution.py:54
  14.1 98.0 %all-to-all-start = ((bf16[16,4,2,128,128]{4,3,2,1,0:T(8,128)(2,1)}), bf16[16,4,2,128,128]{4,3,2,1,0:T(8,128)(2,1)}, u32[]{:S(2)}, u32[]{:S(2)}) async-start(bf16[16,4,2,128,128]{4,3,2,1,0:T(8,128)(2,1)} %bitcast.134), calls=%async_computation | async-start | bytes 8388608 | tf_op jit(solution)/shard_map/all_to_all | solution.py:70
  22.7 5.4 %copy-start.9 = (s32[1,16,4]{1,2,0:T(4,128)S(1)}, s32[1,16,4]{1,2,0:T(4,128)}, u32[]{:S(2)}) copy-start(s32[1,16,4]{1,2,0:T(4,128)} %param.17) | copy-start | bytes 772
  22.8 5.6 %copy-start.12 = (u32[128]{0:T(128)S(1)}, u32[128]{0:T(128)}, u32[]{:S(2)}) copy-start(u32[128]{0:T(128)} %constant.43) | copy-start | bytes 1540
  22.8 7.5 %copy-start.3 = (s32[8]{0:T(128)S(1)}, s32[8]{0:T(128)}, u32[]{:S(2)}) copy-start(s32[8]{0:T(128)} %param.13) | copy-start | bytes 100
  22.8 8.1 %copy-start.7 = (s32[64]{0:T(128)S(1)}, s32[64]{0:T(128)}, u32[]{:S(2)}) copy-start(s32[64]{0:T(128)} %param.14) | copy-start | bytes 772
  22.8 8.1 %copy-start.11 = (s32[64]{0:T(128)S(1)}, s32[64]{0:T(128)}, u32[]{:S(2)}) copy-start(s32[64]{0:T(128)} %param.15) | copy-start | bytes 772
  22.8 12.9 %copy-start.6 = (bf16[32,512]{1,0:T(8,128)(2,1)S(1)}, bf16[32,512]{1,0:T(8,128)(2,1)}, u32[]{:S(2)}) copy-start(bf16[32,512]{1,0:T(8,128)(2,1)} %param.9) | copy-start | bytes 98308
  22.8 307.1 %all-reduce.3.cloned.1.call-start = ((), (), s32[]{:S(2)}) async-start(), calls=%async_computation.2 | async-start | bytes 131072 | tf_op jit(solution)/shard_map/psum | solution.py:120
  29.6 97.4 %copy-start.8 = (f32[64]{0:T(128)}, f32[64]{0:T(128)S(1)}, u32[]{:S(2)}) copy-start(f32[64]{0:T(128)S(1)} %negate_power_fusion) | copy-start | bytes 772
  111.8 15.2 %copy-start.5 = (f32[8,4]{1,0:T(8,128)}, f32[8,4]{1,0:T(8,128)S(1)}, u32[]{:S(2)}) copy-start(f32[8,4]{1,0:T(8,128)S(1)} %add_convert_fusion.1) | copy-start | bytes 388
  201.8 0.8 copy-start.1
  201.8 0.8 copy-start.2
  238.6 2.1 copy-start.4
  243.4 36.9 %copy-start.10 = (pred[4,4]{1,0:T(4,128)(4,1)S(1)}, pred[4,4]{1,0:T(4,128)(4,1)}, u32[]{:S(2)}) copy-start(pred[4,4]{1,0:T(4,128)(4,1)} %iota_compare_fusion.3) | copy-start | bytes 52
Sparse Core Ops, SparseCore 0:
  10.1 182.6 all-gather.1
  247.2 82.6 all-reduce.2
where the time goes:
time: 365 us; the launch traced here: 361 us
  blocking collectives  159 us (44%)
  waiting for transfers between devices  116 us (32%)
  local copies, waits for them, and re-layouts  34.4 us (9%)
  matrix products  19.4 us (5%)
  between operations  15.1 us (4%)
  other arithmetic  9.37 us (3%)
  starting transfers between devices  8.73 us (2%)
    all_gather x1, blocking collectives, body(): full_rows = lax.all_gather(normed, 'seq', axis=1, tiled=True)  76 us
    all_gather x1, waiting for transfers between devices, body(): lax.all_gather(qkv_weight, 'seq', axis=0, tiled=True)  65.8 us
    psum x1, waiting for transfers between devices, body(): lax.psum((request_acc * adjust[:, :, None]).astype(jnp.bfloat16), 'seq')  49.3 us
    pmax x1, blocking collectives, body(): total_max = lax.pmax(request_max, 'seq')  30.9 us
    psum x1, blocking collectives, body(): lax.psum((request_sum * adjust).astype(jnp.bfloat16), 'seq')  29 us
    unnamed x1, blocking collectives  22.7 us
    scatter x1, local copies, waits for them, and re-layouts, body(): jnp.zeros_like(kv_cache).at[recv_list.reshape(-1)]  11.8 us
    dot_general x1, matrix products, body(): jnp.dot(full_rows, lax.all_gather(qkv_weight, 'seq', axis=0, tiled=True),...  8.79 us
  transfers between devices with their start and end apart: 3, of which 2 were waited for; matrix products, arithmetic and copies ran while one was open for 10% of the time, Pallas kernels for 0%

commit v1 on v0

--- a/solution.py
+++ b/solution.py
@@ -48,11 +48,8 @@
     scale_factor = HEAD ** (-0.5)
     requests = lengths.shape[0]
     slot_count = kv_cache.shape[0]
-    full_rows = lax.all_gather(normed, "seq", axis=1, tiled=True)
-    projected_qkv = jnp.dot(
-        full_rows,
-        lax.all_gather(qkv_weight, "seq", axis=0, tiled=True),
-        preferred_element_type=jnp.float32,
+    projected_qkv = lax.psum(
+        jnp.dot(normed, qkv_weight, preferred_element_type=jnp.float32), "seq"
     )
     projected_qkv = projected_qkv.reshape(requests, POS, -1, group_size + 2, HEAD)
     local_kv = projected_qkv.shape[2]

time: 365 us -> 310 us (0.85)
  blocking collectives: 159 us -> 83 us
  waiting for transfers between devices: 116 us -> 140 us
  matrix products: 19.4 us -> 11.7 us
    psum x0 -> x1, waiting for transfers between devices: none -> 90.2 us  [body(): lax.psum(jnp.dot(normed, qkv_weight, preferred_element_type=jnp.float32),...]
    all_gather x1 -> x0, blocking collectives: 76 us -> none  [body(): full_rows = lax.all_gather(normed, 'seq', axis=1, tiled=True)]
    all_gather x1 -> x0, waiting for transfers between devices: 65.8 us -> none  [body(): lax.all_gather(qkv_weight, 'seq', axis=0, tiled=True)]
    dot_general x1, matrix products: 8.79 us -> 1.08 us  [body(): jnp.dot(normed, qkv_weight, preferred_element_type=jnp.float32)]
    unnamed x30 -> x28, local copies, waits for them, and re-layouts: 6.65 us -> 7.41 us
  transfers between devices with their start and end apart: 3 -> 3, of which waited for: 2 -> 2; matrix products, arithmetic and copies ran while one was open for 10% -> 14% of each run, Pallas kernels for 0% -> 0%
where the time goes in v1:
time: 310 us; the launch traced here: 307 us
  waiting for transfers between devices  140 us (45%)
  blocking collectives  83 us (27%)
  local copies, waits for them, and re-layouts  36.8 us (12%)
  between operations  15 us (5%)
  matrix products  11.7 us (4%)
  other arithmetic  11.5 us (4%)
  starting transfers between devices  8.87 us (3%)
    psum x1, waiting for transfers between devices, body(): lax.psum(jnp.dot(normed, qkv_weight, preferred_element_type=jnp.float32),...  90.2 us
    psum x1, waiting for transfers between devices, body(): lax.psum((request_acc * adjust[:, :, None]).astype(jnp.bfloat16), 'seq')  50.1 us
    pmax x1, blocking collectives, body(): total_max = lax.pmax(request_max, 'seq')  31.2 us
    psum x1, blocking collectives, body(): lax.psum((request_sum * adjust).astype(jnp.bfloat16), 'seq')  29.1 us
    unnamed x1, blocking collectives  22.7 us
    scatter x1, local copies, waits for them, and re-layouts, body(): jnp.zeros_like(kv_cache).at[recv_list.reshape(-1)]  12.2 us
    all_to_all x1, starting transfers between devices, body(): lax.all_to_all(outgoing, 'seq', split_axis=0, concat_axis=0, tiled=True)  8.79 us
    unnamed x28, local copies, waits for them, and re-layouts  7.41 us
  transfers between devices with their start and end apart: 3, of which 2 were waited for; matrix products, arithmetic and copies ran while one was open for 14% of the time, Pallas kernels for 0%

profile of v1, /device:TPU:1, one launch (start us, length us, event | category | flops | bytes accessed | tf_op | source)
XLA Modules:
  0.0 307.2 jit_solution(8574549953733495457)
XLA Ops:
  7.2 1.3 copy-done
  8.5 1.1 fusion.56
  9.6 0.7 reshape.410
  10.3 0.7 broadcast_minimum_fusion
  11.2 5.2 %gather_fusion.2 = bf16[64,2,128,128]{3,2,1,0:T(8,128)(2,1)} fusion(bf16[64,2,128,128]{3,2,1,0:T(8,128)(2,1)} %param.12, s32[1024]{0:T(1024)S(1)} %pad_clamp_fusion), kind=kCustom, calls=%fused_computation.2 | custom fusion | bytes 8388864 | tf_op jit(solution)/shard_map/gather | solution.py:65
  16.5 8.8 %all-to-all-start = ((bf16[16,4,2,128,128]{4,3,2,1,0:T(8,128)(2,1)}), bf16[16,4,2,128,128]{4,3,2,1,0:T(8,128)(2,1)}, u32[]{:S(2)}, u32[]{:S(2)}) async-start(bf16[16,4,2,128,128]{4,3,2,1,0:T(8,128)(2,1)} %bitcast.131), calls=%async_computation | async-start | bytes 8388608 | tf_op jit(solution)/shard_map/all_to_all | solution.py:67
  25.5 0.7 fusion.53
  26.3 0.6 fusion.49
  26.9 0.2 multiply_cosine_fusion.1
  27.1 4.9 %compare_select_fusion.3 = (s32[64]{0:T(128)S(1)}, s32[64]{0:T(128)S(1)}, s32[64]{0:T(128)S(1)}) fusion(s32[]{:T(128)} %bitcast.1, s32[]{:T(128)} %bitcast.2, s32[]{:T(128)} %bitcast.3, s32[]{:T(128)} %bitcast.4, s32[]{:T(128)} %bitcast.5, s32[]{:T(128)} %bitcast.6, s32[]{:T(128)} %bitcast.7, s32[]{:T(128)} %bitcast.8, s32[64]{0:T(128)S(1)} %copy-done.6, ...), kind=kLoop, calls=%fused_computation.87 | loop fusion | flops 1216 | bytes 1312 | tf_op jit(solution)/shard_map/gather | solution.py:73
  32.0 0.1 fusion.31
  32.1 0.5 iota_compare_fusion.3
  32.6 4.8 %copy.107 = bf16[64,2,128,128]{3,2,0,1:T(8,128)(2,1)} copy(bf16[64,2,128,128]{3,2,1,0:T(8,128)(2,1)} %param.12) | data formatting | bytes 8388608 | tf_op args[3]
  37.5 0.6 dynamic-slice
  38.7 90.2 %all-reduce.4.cloned.1.call-done = f32[8,4,1,10,128]{4,3,1,0,2:T(8,128)} async-done(((f32[8,4,1,10,128]{4,3,1,0,2:T(8,128)}), f32[8,4,1,10,128]{4,3,1,0,2:T(8,128)}) %all-reduce.4.cloned.1.call-update) | async-done | bytes 163856 | tf_op jit(solution)/shard_map/psum | solution.py:51
  128.9 1.1 subtract_convert_fusion
  130.0 0.1 maximum_bitcast_fusion
  130.1 0.7 gather_fusion
  130.8 2.9 fusion.54
  133.8 0.8 fusion.15
  134.6 2.3 fusion
  136.9 0.4 reshape.416
  137.3 0.7 copy.64
  138.0 0.1 select_reduce_fusion
  138.2 0.6 gather_fusion.1
  138.8 31.2 %pmax.7 = f32[8,32]{1,0:T(8,128)S(1)} all-reduce(f32[8,32]{1,0:T(8,128)S(1)} %bitcast.130), channel_id=1, replica_groups=mesh['seq'=16,'head'=8] {'seq'}, use_global_device_ids=true, to_apply=%region_3.4 | all-reduce | flops 256 | bytes 2048 | tf_op jit(solution)/shard_map/pmax | solution.py:113
  170.2 0.7 copy.66
  170.9 0.7 copy.74
  171.6 0.8 subtract_exponential_fusion
  172.3 0.9 fusion.11
  173.2 0.1 copy.75
  173.3 0.1 copy.76
  173.4 0.3 mul.180
  173.8 1.8 fusion.7
  175.6 0.7 copy.67
  176.3 0.9 slice.55
  177.2 0.9 fusion.45
  178.1 1.3 fusion.55
  179.4 29.1 %psum.23 = bf16[8,8,4]{1,2,0:T(4,128)(2,1)S(1)} all-reduce(bf16[8,8,4]{1,2,0:T(4,128)(2,1)S(1)} %copy.76), channel_id=1, replica_groups=mesh['seq'=16,'head'=8] {'seq'}, use_global_device_ids=true, to_apply=%region_7.8 | all-reduce | flops 256 | bytes 1024 | tf_op jit(solution)/shard_map/psum | solution.py:116
  208.5 0.7 fusion.24
  209.3 0.9 slice.88
  210.2 50.1 %all-reduce.6.cloned.1.call-done = bf16[8,8,4,128]{3,1,2,0:T(8,128)(2,1)} async-done(((bf16[8,8,4,128]{3,1,2,0:T(8,128)(2,1)}), bf16[8,8,4,128]{3,1,2,0:T(8,128)(2,1)}) %all-reduce.6.cloned.1.call-update) | async-done | bytes 65552 | tf_op jit(solution)/shard_map/psum | solution.py:117
  260.3 1.1 fusion.8
  261.4 0.3 convolution_convert_fusion
  261.7 22.7 %all-reduce = bf16[32,512]{1,0:T(8,128)(2,1)S(1)} all-reduce(bf16[32,512]{1,0:T(8,128)(2,1)S(1)} %convolution_convert_fusion), channel_id=2, replica_groups=mesh['seq'=16,'head'=8] {'head'}, use_global_device_ids=true, to_apply=%region_9.10.clone | all-reduce | flops 16384 | bytes 65536
  284.4 0.6 constant_dynamic-slice_fusion
  285.0 3.1 broadcast_in_dim.96
  288.1 12.2 %scatter_fusion = bf16[64,2,128,128]{3,2,1,0:T(8,128)(2,1)} fusion(bf16[64,2,128,128]{3,2,1,0:T(8,128)(2,1)} %broadcast_in_dim.96, s32[64]{0:T(128)S(1)} %copy-done.9, bf16[64,2,128,128]{3,2,1,0:T(8,128)(2,1)} %bitcast.45), kind=kCustom, calls=%fused_computation.3 | custom fusion | bytes 12583168 | tf_op jit(solution)/shard_map/scatter | solution.py:69
  (48 shorter events, 1.0 us)
Async XLA Ops:
  7.2 1.3 copy-start
  7.2 121.7 %all-reduce.4.cloned.1.call-start = ((), (), s32[]{:S(2)}) async-start(), calls=%async_computation.1 | async-start | bytes 524288 | tf_op jit(solution)/shard_map/psum | solution.py:51
  16.5 8.9 %copy-start.6 = (s32[64]{0:T(128)S(1)}, s32[64]{0:T(128)}, u32[]{:S(2)}) copy-start(s32[64]{0:T(128)} %param.14) | copy-start | bytes 772
  16.5 8.9 %copy-start.3 = (s32[8]{0:T(128)S(1)}, s32[8]{0:T(128)}, u32[]{:S(2)}) copy-start(s32[8]{0:T(128)} %param.13) | copy-start | bytes 100
  16.5 9.7 %copy-start.8 = (s32[1,16,4]{1,2,0:T(4,128)S(1)}, s32[1,16,4]{1,2,0:T(4,128)}, u32[]{:S(2)}) copy-start(s32[1,16,4]{1,2,0:T(4,128)} %param.17) | copy-start | bytes 772
  16.5 10.6 %copy-start.10 = (s32[64]{0:T(128)S(1)}, s32[64]{0:T(128)}, u32[]{:S(2)}) copy-start(s32[64]{0:T(128)} %param.15) | copy-start | bytes 772
  16.5 268.5 %all-to-all-start = ((bf16[16,4,2,128,128]{4,3,2,1,0:T(8,128)(2,1)}), bf16[16,4,2,128,128]{4,3,2,1,0:T(8,128)(2,1)}, u32[]{:S(2)}, u32[]{:S(2)}) async-start(bf16[16,4,2,128,128]{4,3,2,1,0:T(8,128)(2,1)} %bitcast.131), calls=%async_computation | async-start | bytes 8388608 | tf_op jit(solution)/shard_map/all_to_all | solution.py:67
  25.3 235.0 %all-reduce.6.cloned.1.call-start = ((), (), s32[]{:S(2)}) async-start(), calls=%async_computation.2 | async-start | bytes 131072 | tf_op jit(solution)/shard_map/psum | solution.py:117
  25.4 12.1 %copy-start.7 = (f32[64]{0:T(128)}, f32[64]{0:T(128)S(1)}, u32[]{:S(2)}) copy-start(f32[64]{0:T(128)S(1)} %negate_power_fusion) | copy-start | bytes 772
  25.5 12.0 %copy-start.5 = (f32[8,4]{1,0:T(8,128)}, f32[8,4]{1,0:T(8,128)S(1)}, u32[]{:S(2)}) copy-start(f32[8,4]{1,0:T(8,128)S(1)} %add_convert_fusion.1) | copy-start | bytes 388
  32.6 4.8 %copy-start.11 = (u32[128]{0:T(128)S(1)}, u32[128]{0:T(128)}, u32[]{:S(2)}) copy-start(u32[128]{0:T(128)} %constant.43) | copy-start | bytes 1540
  130.0 0.8 copy-start.2
  170.2 0.7 copy-start.4
  170.2 91.2 %copy-start.1 = (bf16[1024,512]{1,0:T(8,128)(2,1)S(1)}, bf16[1024,512]{1,0:T(8,128)(2,1)}, u32[]{:S(2)}) copy-start(bf16[1024,512]{1,0:T(8,128)(2,1)} %param.11) | copy-start | bytes 3145732
  175.6 112.5 %copy-start.9 = (s32[64]{0:T(128)S(1)}, s32[64]{0:T(128)}, u32[]{:S(2)}) copy-start(s32[64]{0:T(128)} %fusion.49) | copy-start | bytes 772
Sparse Core Ops, SparseCore 0:
  11.2 117.6 all-reduce.3
  176.4 83.8 all-reduce.5
